TPU v7x, 256 devices: a whole 4x4x8 slice. The times are simulated.
256 devices in a mesh: row: 8 (over z), col: 4 (over x_hi, core), chan: 8 (over x_lo, y).
Axes of the slice: x: 4 (x_hi: 2, x_lo: 2; x = x_hi * 2 + x_lo), y: 4, z: 8, core: 2. Of those that a mesh axis runs over, the one named last changes fastest.
Arguments:
- alignment_features: bfloat16 [2048, 512, 64], P('col', 'row'), may hold values from -8 to 8
- alignment_row_mask: int32 [2048], P('col'), may hold values 0 or 1
- residue_token_mask: int32 [512], P('row'), may hold values 0 or 1
- layer_norm_gain: float32 [64], replicated, may hold values from 0.25 to 1.75
- layer_norm_bias: float32 [64], replicated, may hold values from -3 to 3
- left_factor_weight: bfloat16 [64, 32], P(None, 'chan'), may hold values from -0.75 to 0.75
- right_factor_weight: bfloat16 [64, 32], replicated, may hold values from -0.75 to 0.75
- output_weight: bfloat16 [1024, 128], P('chan'), may hold values from -0.1875 to 0.1875
- output_bias: float32 [128], replicated, may hold values from -3 to 3
Outputs:
- pair_update: bfloat16 [512, 512, 128], P('col', ('row', 'chan'))
All inputs are finite; a program needn't handle non-finite values. No bound on the sum of `alignment_row_mask` or of `residue_token_mask` on one device may be relied on, other than what follows from the above.
Results may differ from a plain program's by a relative error of at most 0.0038.
Values may be sent and summed in bfloat16 or wider, within the bound.
No kernel may reach another device: no remote copies, remote signals or barrier semaphores. Data moves between devices by JAX's collectives and lax.ppermute only.
A program may use at most 128 MiB of HBM per device.

v0:
```python
import jax
import jax.numpy as jnp
from jax import lax
from jax.sharding import PartitionSpec as P


def apply_layer_norm(features, layer_norm_gain, layer_norm_bias):
    values = features.astype(jnp.float32)
    center = values - jnp.mean(values, axis=-1, keepdims=True)
    spread = jnp.mean(center * center, axis=-1, keepdims=True)
    return (center * lax.rsqrt(spread + 1e-05) * layer_norm_gain + layer_norm_bias).astype(
        jnp.bfloat16
    )


def make_factors(
    features,
    rows_used,
    tokens_used,
    layer_norm_gain,
    layer_norm_bias,
    left_factor_weight,
    right_factor_weight,
):
    normalized_features = apply_layer_norm(features, layer_norm_gain, layer_norm_bias)
    weight = rows_used[:, None].astype(jnp.float32) * tokens_used[None, :].astype(jnp.float32)
    left_part = (
        jnp.einsum(
            "stm,mc->sct",
            normalized_features,
            left_factor_weight,
            preferred_element_type=jnp.float32,
        )
        * weight[:, None, :]
    )
    right_part = (
        jnp.einsum(
            "stm,me->ste",
            normalized_features,
            right_factor_weight,
            preferred_element_type=jnp.float32,
        )
        * weight[:, :, None]
    )
    return (left_part.astype(jnp.bfloat16), right_part.astype(jnp.bfloat16))


def body(
    alignment_features,
    alignment_row_mask,
    residue_token_mask,
    layer_norm_gain,
    layer_norm_bias,
    left_factor_weight,
    right_factor_weight,
    output_weight,
    output_bias,
):
    every_feature, every_row = (
        lax.all_gather(alignment_features, "col", axis=0, tiled=True),
        lax.all_gather(alignment_row_mask, "col", axis=0, tiled=True),
    )
    left_part, right_every = make_factors(
        every_feature,
        every_row,
        residue_token_mask,
        layer_norm_gain,
        layer_norm_bias,
        left_factor_weight,
        right_factor_weight,
    )
    tokens_here = residue_token_mask.shape[0]
    mask_shaped = residue_token_mask.reshape(1, 1, tokens_here)
    owner_count = lax.axis_size("row") // lax.axis_size("col")
    block_tokens = tokens_here * owner_count
    col_index = lax.axis_index("col")
    left_every, mask_every = (
        lax.all_gather(left_part, "row", axis=2, tiled=True),
        lax.all_gather(mask_shaped, "row", axis=2, tiled=True),
    )
    left_block = lax.dynamic_slice_in_dim(left_every, col_index * block_tokens, block_tokens, 2)
    mask_block = lax.dynamic_slice_in_dim(mask_every, col_index * block_tokens, block_tokens, 2)
    products = jnp.einsum(
        "sci,sje->ijce", left_block, right_every, preferred_element_type=jnp.float32
    ).astype(jnp.bfloat16)
    flat_products = products.reshape(block_tokens * tokens_here, -1)
    partial_pairs = jnp.dot(
        flat_products, output_weight, preferred_element_type=jnp.float32
    ).reshape(block_tokens, tokens_here, -1)
    chan_count = lax.axis_size("chan")
    share = tokens_here // chan_count
    chan_index = lax.axis_index("chan")
    total_pairs = lax.psum(partial_pairs, "chan")
    summed = lax.dynamic_slice_in_dim(total_pairs, chan_index * share, share, 1)
    row_total = jnp.sum(every_row).astype(jnp.float32)
    first_used = mask_block.reshape(block_tokens).astype(jnp.float32)
    second_used = lax.dynamic_slice_in_dim(residue_token_mask, chan_index * share, share, 0).astype(
        jnp.float32
    )
    count = jnp.maximum(row_total * first_used[:, None] * second_used[None, :], 1.0)
    return ((summed + output_bias) / count[:, :, None]).astype(jnp.bfloat16)


def solution(mesh):
    in_specs = (
        P("col", "row", None),
        P("col"),
        P("row"),
        P(),
        P(),
        P(None, "chan"),
        P(),
        P("chan", None),
        P(),
    )
    out_specs = P("col", ("row", "chan"), None)
    return jax.shard_map(body, mesh=mesh, in_specs=in_specs, out_specs=out_specs, check_vma=False)
```

profile of v0, /device:TPU:1, one launch (start us, length us, event | category | flops | bytes accessed | tf_op | source)
XLA Modules:
  0.0 390.0 jit_solution(13971857495411139468)
XLA Ops:
  6.5 0.7 all-gather.5.cloned.1.call-update
  7.3 0.0 all-gather.7.cloned.1.call-start
  7.3 0.7 convert_element_type.49
  8.0 9.9 %all-gather.1 = s32[4,1,512]{2,1,0:T(1,128)S(1)} all-gather(s32[1,1,512]{2,1,0:T(1,128)} %bitcast.35), channel_id=1, replica_groups=mesh['row'=8,'col'=4,'chan'=8] {'col'}, dimensions={0}, use_global_device_ids=true | all-gather | bytes 10240 | tf_op jit(solution)/shard_map/all_gather | solution.py:61
  17.8 0.6 fusion.25
  18.5 0.1 broadcast_multiply_fusion
  18.6 0.0 copy-start.4
  18.6 107.3 %all-gather.5.cloned.1.call-done = bf16[2048,64,64]{0,2,1:T(8,128)(2,1)} async-done(((bf16[512,64,64]{0,2,1:T(8,128)(2,1)}), bf16[2048,64,64]{0,2,1:T(8,128)(2,1)}) %all-gather.5.cloned.1.call-update) | async-done | bytes 16777232 | tf_op jit(solution)/shard_map/all_gather | solution.py:60
  125.9 7.4 %convert_reduce_fusion = f32[2048,64]{0,1:T(8,128)S(1)} fusion(bf16[2048,64,64]{0,2,1:T(8,128)(2,1)} %all-gather.5.cloned.1.call-done), kind=kLoop, calls=%fused_computation.1 | loop fusion | flops 16646144 | bytes 17301504 | tf_op jit(solution)/shard_map/reduce_sum | solution.py:9
  133.3 3.2 copy-done.1
  136.5 5.4 %fusion.2 = f32[2048,64]{0,1:T(8,128)S(1)} fusion(bf16[2048,64,64]{0,2,1:T(8,128)(2,1)S(1)} %copy-done.1, f32[2048,64]{0,1:T(8,128)S(1)} %broadcast_multiply_fusion.1), kind=kLoop, calls=%fused_computation.4 | loop fusion | flops 33423360 | bytes 17825792 | tf_op jit(solution)/shard_map/reduce_sum | solution.py:10
  141.9 0.1 add_rsqrt_fusion
  142.0 6.6 %fusion.5 = bf16[2048,64,64]{0,2,1:T(8,128)(2,1)S(1)} fusion(bf16[2048,64,64]{0,2,1:T(8,128)(2,1)S(1)} %copy-done.1, f32[64]{0:T(128)S(1)} %copy-done.4, f32[64]{0:T(128)S(1)} %copy-done.5, f32[2048,64]{0,1:T(8,128)S(1)} %add_rsqrt_fusion, f32[2048,64]{0,1:T(8,128)S(1)} %broadcast_multiply_fusion.1), kind=kLoop, calls=%fused_computation.7 | loop fusion | flops 50331648 | bytes 34603520 | tf_op jit(solution)/shard_map/convert_element_type | solution.py:11
  148.7 5.7 %copy-done.2 = bf16[2048,64,64]{0,2,1:T(8,128)(2,1)} copy-done((bf16[2048,64,64]{0,2,1:T(8,128)(2,1)}, bf16[2048,64,64]{0,2,1:T(8,128)(2,1)S(1)}, u32[]{:S(2)}) %copy-start.2) | copy-done | bytes 16777240
  154.4 5.2 %fusion.13 = bf16[2048,4,64]{0,1,2:T(4,128)(2,1)} fusion(bf16[2048,64,64]{0,2,1:T(8,128)(2,1)S(1)} %fusion.5, f32[2048,64]{0,1:T(8,128)S(1)} %broadcast_multiply_fusion, bf16[64,4]{0,1:T(4,128)(2,1)S(1)} %copy-done.3), kind=kOutput, calls=%fused_computation.15 | convolution fusion | flops 68157440 | bytes 18350592 | tf_op jit(solution)/shard_map/stm,mc->sct/dot_general | solution.py:28
  159.6 0.0 all-gather.7.cloned.1.call-update
  159.6 0.0 all-reduce.3.cloned.1.call-start
  159.7 93.1 %all-gather.7.cloned.1.call-done = bf16[2048,4,512]{0,1,2:T(4,128)(2,1)} async-done(((bf16[2048,4,64]{0,1,2:T(4,128)(2,1)}), bf16[2048,4,512]{0,1,2:T(4,128)(2,1)}) %all-gather.7.cloned.1.call-update) | async-done | bytes 8388624 | tf_op jit(solution)/shard_map/all_gather | solution.py:78
  252.7 2.6 constant_dynamic-slice_fusion
  255.3 3.0 copy.18
  258.4 11.0 %fusion.15 = bf16[64,32,4,128]{3,1,2,0:T(8,128)(2,1)S(1)} fusion(bf16[2048,4,128]{2,0,1:T(8,128)(2,1)} %copy.18, f32[2048,64]{0,1:T(8,128)S(1)} %broadcast_multiply_fusion, bf16[2048,64,64]{0,2,1:T(8,128)(2,1)} %copy-done.2, bf16[64,32]{0,1:T(8,128)(2,1)S(1)} %copy-done.7), kind=kOutput, calls=%fused_computation.17 | convolution fusion | flops 4841275392 | bytes 21499904 | tf_op jit(solution)/shard_map/sci,sje->ijce/dot_general | solution.py:83
  269.4 2.7 fusion.20
  272.2 0.0 all-reduce.3.cloned.1.call-update
  272.9 0.6 dynamic-slice.1
  274.1 0.2 dynamic-update-slice
  274.4 9.1 %all-reduce = s32[512]{0:T(512)S(1)} all-reduce(s32[512]{0:T(512)S(1)} %dynamic-update-slice), channel_id=2, replica_groups=mesh['row'=8,'col'=4,'chan'=8] {'row'}, use_global_device_ids=true, to_apply=%add | all-reduce | flops 512 | bytes 4096
  283.5 0.1 dynamic-slice_convert_fusion
  283.5 0.1 convert_multiply_fusion
  283.6 0.1 multiply_maximum_fusion
  283.7 97.7 %all-reduce.3.cloned.1.call-done = f32[128,64,128]{2,0,1:T(8,128)} async-done(((f32[128,64,128]{2,0,1:T(8,128)}), f32[128,64,128]{2,0,1:T(8,128)}) %all-reduce.3.cloned.1.call-update) | async-done | bytes 4194320 | tf_op jit(solution)/shard_map/psum | solution.py:93
  381.3 1.2 divide_convert_fusion
  382.6 0.9 copy.15
  (20 shorter events, 0.1 us)
Async XLA Ops:
  6.5 262.9 %copy-start = (bf16[128,128]{1,0:T(8,128)(2,1)S(1)}, bf16[128,128]{1,0:T(8,128)(2,1)}, u32[]{:S(2)}) copy-start(bf16[128,128]{1,0:T(8,128)(2,1)} %param.16) | copy-start | bytes 98308
  6.5 119.3 %all-gather.5.cloned.1.call-start = ((), (), s32[]{:S(2)}) async-start(), calls=%async_computation | async-start | bytes 20971520 | tf_op jit(solution)/shard_map/all_gather | solution.py:60
  7.3 245.5 %all-gather.7.cloned.1.call-start = ((), (), s32[]{:S(2)}) async-start(), calls=%async_computation.1 | async-start | bytes 9437184 | tf_op jit(solution)/shard_map/all_gather | solution.py:78
  18.6 123.4 %copy-start.4 = (f32[64]{0:T(128)S(1)}, f32[64]{0:T(128)}, u32[]{:S(2)}) copy-start(f32[64]{0:T(128)} %param.13) | copy-start | bytes 772
  18.6 123.4 %copy-start.5 = (f32[64]{0:T(128)S(1)}, f32[64]{0:T(128)}, u32[]{:S(2)}) copy-start(f32[64]{0:T(128)} %param.12) | copy-start | bytes 772
  125.9 10.7 %copy-start.1 = (bf16[2048,64,64]{0,2,1:T(8,128)(2,1)S(1)}, bf16[2048,64,64]{0,2,1:T(8,128)(2,1)}, u32[]{:S(2)}) copy-start(bf16[2048,64,64]{0,2,1:T(8,128)(2,1)} %all-gather.5.cloned.1.call-done) | copy-start | bytes 50331652
  142.0 12.4 %copy-start.3 = (bf16[64,4]{0,1:T(4,128)(2,1)S(1)}, bf16[64,4]{0,1:T(4,128)(2,1)}, u32[]{:S(2)}) copy-start(bf16[64,4]{0,1:T(4,128)(2,1)} %param.14) | copy-start | bytes 1540
  148.7 5.7 %copy-start.2 = (bf16[2048,64,64]{0,2,1:T(8,128)(2,1)}, bf16[2048,64,64]{0,2,1:T(8,128)(2,1)S(1)}, u32[]{:S(2)}) copy-start(bf16[2048,64,64]{0,2,1:T(8,128)(2,1)S(1)} %fusion.5) | copy-start | bytes 50331652
  154.4 104.0 %copy-start.7 = (bf16[64,32]{0,1:T(8,128)(2,1)S(1)}, bf16[64,32]{0,1:T(8,128)(2,1)}, u32[]{:S(2)}) copy-start(bf16[64,32]{0,1:T(8,128)(2,1)} %param.15) | copy-start | bytes 12292
  159.6 221.7 %all-reduce.3.cloned.1.call-start = ((), (), s32[]{:S(2)}) async-start(), calls=%async_computation.2 | async-start | bytes 8388608 | tf_op jit(solution)/shard_map/psum | solution.py:93
  258.4 14.5 %copy-start.9 = (u32[256]{0:T(256)S(1)}, u32[256]{0:T(256)}, u32[]{:S(2)}) copy-start(u32[256]{0:T(256)} %constant.32) | copy-start | bytes 3076
  258.4 15.7 %copy-start.8 = (s32[64]{0:T(128)S(1)}, s32[64]{0:T(128)}, u32[]{:S(2)}) copy-start(s32[64]{0:T(128)} %param.11) | copy-start | bytes 772
  258.4 123.0 %copy-start.6 = (f32[128]{0:T(128)S(1)}, f32[128]{0:T(128)}, u32[]{:S(2)}) copy-start(f32[128]{0:T(128)} %param.17) | copy-start | bytes 1540
Sparse Core Ops, SparseCore 0:
  9.1 116.6 all-gather.4
  159.7 92.9 all-gather.6
  272.3 108.9 all-reduce.2
where the time goes:
time: 390 us
  waiting for transfers between devices  299 us (77%)
  other arithmetic  22.4 us (6%)
  blocking collectives  19 us (5%)
  matrix products  19 us (5%)
  local copies, waits for them, and re-layouts  16.3 us (4%)
  between operations  14.6 us (4%)
    all_gather x1, waiting for transfers between devices, body(): lax.all_gather(alignment_features, 'col', axis=0, tiled=True)  107 us
    psum x1, waiting for transfers between devices, body(): total_pairs = lax.psum(partial_pairs, 'chan')  97.7 us
    all_gather x1, waiting for transfers between devices, body(): lax.all_gather(left_part, 'row', axis=2, tiled=True)  93.1 us
    unnamed x24, local copies, waits for them, and re-layouts  12.8 us
    dot_general x1, matrix products, body(): jnp.einsum('sci,sje->ijce', left_block, right_every, preferred_element_ty...  11 us
    all_gather x1, blocking collectives, body(): lax.all_gather(alignment_row_mask, 'col', axis=0, tiled=True)  9.85 us
    unnamed x1, blocking collectives  9.1 us
  transfers between devices with their start and end apart: 3, of which 3 were waited for; matrix products, arithmetic and copies ran while one was open for 1% of the time, Pallas kernels for 0%

commit v1 on v0

--- a/solution.py
+++ b/solution.py
@@ -90,7 +90,7 @@
     chan_count = lax.axis_size("chan")
     share = tokens_here // chan_count
     chan_index = lax.axis_index("chan")
-    total_pairs = lax.psum(partial_pairs, "chan")
+    total_pairs = jnp.sum(lax.all_gather(partial_pairs, "chan"), axis=0)
     summed = lax.dynamic_slice_in_dim(total_pairs, chan_index * share, share, 1)
     row_total = jnp.sum(every_row).astype(jnp.float32)
     first_used = mask_block.reshape(block_tokens).astype(jnp.float32)

time: 390 us -> 624 us (1.60)
  waiting for transfers between devices: 299 us -> 519 us
  other arithmetic: 22.4 us -> 36.6 us
    all_gather x0 -> x1, waiting for transfers between devices: none -> 318 us  [body(): total_pairs = jnp.sum(lax.all_gather(partial_pairs, 'chan'), axis=0)]
    psum x1 -> x0, waiting for transfers between devices: 97.7 us -> none  [body(): total_pairs = lax.psum(partial_pairs, 'chan')]
    reduce_sum x0 -> x1, other arithmetic: none -> 14.2 us  [body(): total_pairs = jnp.sum(lax.all_gather(partial_pairs, 'chan'), axis=0)]
  transfers between devices with their start and end apart: 3 -> 3, of which waited for: 3 -> 3; matrix products, arithmetic and copies ran while one was open for 1% -> 0% of each run, Pallas kernels for 0% -> 0%
where the time goes in v1:
time: 624 us
  waiting for transfers between devices  519 us (83%)
  other arithmetic  36.6 us (6%)
  matrix products  19 us (3%)
  blocking collectives  18.9 us (3%)
  local copies, waits for them, and re-layouts  16.3 us (3%)
  between operations  14.6 us (2%)
    all_gather x1, waiting for transfers between devices, body(): total_pairs = jnp.sum(lax.all_gather(partial_pairs, 'chan'), axis=0)  318 us
    all_gather x1, waiting for transfers between devices, body(): lax.all_gather(alignment_features, 'col', axis=0, tiled=True)  107 us
    all_gather x1, waiting for transfers between devices, body(): lax.all_gather(left_part, 'row', axis=2, tiled=True)  93.1 us
    reduce_sum x1, other arithmetic, body(): total_pairs = jnp.sum(lax.all_gather(partial_pairs, 'chan'), axis=0)  14.2 us
    unnamed x24, local copies, waits for them, and re-layouts  12.8 us
  transfers between devices with their start and end apart: 3, of which 3 were waited for; matrix products, arithmetic and copies ran while one was open for 0% of the time, Pallas kernels for 0%

profile of v1, /device:TPU:1, one launch (start us, length us, event | category | flops | bytes accessed | tf_op | source)
XLA Modules:
  0.0 624.2 jit_solution(3854344990788508232)
XLA Ops:
  6.5 0.7 all-gather.7.cloned.1.call-update
  7.3 0.0 all-gather.9.cloned.1.call-start
  7.3 0.7 convert_element_type.49
  8.0 9.9 %all-gather.2 = s32[4,1,512]{2,1,0:T(1,128)S(1)} all-gather(s32[1,1,512]{2,1,0:T(1,128)} %bitcast.37), channel_id=1, replica_groups=mesh['row'=8,'col'=4,'chan'=8] {'col'}, dimensions={0}, use_global_device_ids=true | all-gather | bytes 10240 | tf_op jit(solution)/shard_map/all_gather | solution.py:61
  17.8 0.6 fusion.25
  18.5 0.1 broadcast_multiply_fusion
  18.6 107.3 %all-gather.7.cloned.1.call-done = bf16[2048,64,64]{0,2,1:T(8,128)(2,1)} async-done(((bf16[512,64,64]{0,2,1:T(8,128)(2,1)}), bf16[2048,64,64]{0,2,1:T(8,128)(2,1)}) %all-gather.7.cloned.1.call-update) | async-done | bytes 16777232 | tf_op jit(solution)/shard_map/all_gather | solution.py:60
  125.9 7.4 %convert_reduce_fusion = f32[2048,64]{0,1:T(8,128)S(1)} fusion(bf16[2048,64,64]{0,2,1:T(8,128)(2,1)} %all-gather.7.cloned.1.call-done), kind=kLoop, calls=%fused_computation.1 | loop fusion | flops 16646144 | bytes 17301504 | tf_op jit(solution)/shard_map/reduce_sum | solution.py:9
  133.3 3.2 copy-done.1
  136.5 5.4 fusion.2
  141.9 0.1 add_rsqrt_fusion
  142.0 6.6 %fusion.5 = bf16[2048,64,64]{0,2,1:T(8,128)(2,1)S(1)} fusion(bf16[2048,64,64]{0,2,1:T(8,128)(2,1)S(1)} %copy-done.1, f32[64]{0:T(128)S(1)} %copy-done.4, f32[64]{0:T(128)S(1)} %copy-done.5, f32[2048,64]{0,1:T(8,128)S(1)} %add_rsqrt_fusion, f32[2048,64]{0,1:T(8,128)S(1)} %broadcast_multiply_fusion.1), kind=kLoop, calls=%fused_computation.7 | loop fusion | flops 50331648 | bytes 34603520 | tf_op jit(solution)/shard_map/convert_element_type | solution.py:11
  148.7 5.7 copy-done.2
  154.4 5.2 fusion.13
  159.6 0.0 all-gather.9.cloned.1.call-update
  159.6 0.0 all-gather.11.cloned.1.call-start
  159.7 93.1 %all-gather.9.cloned.1.call-done = bf16[2048,4,512]{0,1,2:T(4,128)(2,1)} async-done(((bf16[2048,4,64]{0,1,2:T(4,128)(2,1)}), bf16[2048,4,512]{0,1,2:T(4,128)(2,1)}) %all-gather.9.cloned.1.call-update) | async-done | bytes 8388624 | tf_op jit(solution)/shard_map/all_gather | solution.py:78
  252.7 2.6 constant_dynamic-slice_fusion
  255.4 3.0 copy.17
  258.4 11.0 %fusion.15 = bf16[64,32,4,128]{3,1,2,0:T(8,128)(2,1)S(1)} fusion(bf16[2048,4,128]{2,0,1:T(8,128)(2,1)} %copy.17, f32[2048,64]{0,1:T(8,128)S(1)} %broadcast_multiply_fusion, bf16[2048,64,64]{0,2,1:T(8,128)(2,1)} %copy-done.2, bf16[64,32]{0,1:T(8,128)(2,1)S(1)} %copy-done.7), kind=kOutput, calls=%fused_computation.17 | convolution fusion | flops 4841275392 | bytes 21499904 | tf_op jit(solution)/shard_map/sci,sje->ijce/dot_general | solution.py:83
  269.4 2.8 fusion.20
  272.2 0.0 all-gather.11.cloned.1.call-update
  272.9 0.6 dynamic-slice.1
  274.1 0.2 dynamic-update-slice
  274.4 9.1 %all-reduce = s32[512]{0:T(512)S(1)} all-reduce(s32[512]{0:T(512)S(1)} %dynamic-update-slice), channel_id=3, replica_groups=mesh['row'=8,'col'=4,'chan'=8] {'row'}, use_global_device_ids=true, to_apply=%add | all-reduce | flops 512 | bytes 4096
  283.5 0.1 dynamic-slice_convert_fusion
  283.5 0.1 convert_multiply_fusion
  283.6 0.1 multiply_maximum_fusion
  283.7 317.6 %all-gather.11.cloned.1.call-done = f32[1024,64,128]{2,0,1:T(8,128)} async-done(((f32[128,64,128]{2,0,1:T(8,128)}), f32[1024,64,128]{2,0,1:T(8,128)}) %all-gather.11.cloned.1.call-update) | async-done | bytes 33554448 | tf_op jit(solution)/shard_map/all_gather | solution.py:93
  601.3 14.2 %reduce_sum.38 = f32[128,64,128]{2,0,1:T(8,128)} reduce(f32[8,128,64,128]{3,1,0,2:T(8,128)} %bitcast.34, f32[]{:T(128)} %constant.11.clone.1), dimensions={0}, to_apply=%region_2.0 | reduce | flops 7340032 | bytes 37748740 | tf_op jit(solution)/shard_map/reduce_sum | solution.py:93
  615.6 1.2 divide_convert_fusion
  616.8 0.9 copy.14
  (21 shorter events, 0.1 us)
Async XLA Ops:
  6.5 262.8 %copy-start = (bf16[128,128]{1,0:T(8,128)(2,1)S(1)}, bf16[128,128]{1,0:T(8,128)(2,1)}, u32[]{:S(2)}) copy-start(bf16[128,128]{1,0:T(8,128)(2,1)} %param.16) | copy-start | bytes 98308
  6.5 119.3 %all-gather.7.cloned.1.call-start = ((), (), s32[]{:S(2)}) async-start(), calls=%async_computation | async-start | bytes 20971520 | tf_op jit(solution)/shard_map/all_gather | solution.py:60
  7.3 245.5 %all-gather.9.cloned.1.call-start = ((), (), s32[]{:S(2)}) async-start(), calls=%async_computation.1 | async-start | bytes 9437184 | tf_op jit(solution)/shard_map/all_gather | solution.py:78
  18.6 123.4 %copy-start.4 = (f32[64]{0:T(128)S(1)}, f32[64]{0:T(128)}, u32[]{:S(2)}) copy-start(f32[64]{0:T(128)} %param.13) | copy-start | bytes 772
  18.6 123.4 %copy-start.5 = (f32[64]{0:T(128)S(1)}, f32[64]{0:T(128)}, u32[]{:S(2)}) copy-start(f32[64]{0:T(128)} %param.12) | copy-start | bytes 772
  125.9 10.7 %copy-start.1 = (bf16[2048,64,64]{0,2,1:T(8,128)(2,1)S(1)}, bf16[2048,64,64]{0,2,1:T(8,128)(2,1)}, u32[]{:S(2)}) copy-start(bf16[2048,64,64]{0,2,1:T(8,128)(2,1)} %all-gather.7.cloned.1.call-done) | copy-start | bytes 50331652
  142.0 12.4 %copy-start.3 = (bf16[64,4]{0,1:T(4,128)(2,1)S(1)}, bf16[64,4]{0,1:T(4,128)(2,1)}, u32[]{:S(2)}) copy-start(bf16[64,4]{0,1:T(4,128)(2,1)} %param.14) | copy-start | bytes 1540
  148.7 5.7 copy-start.2
  154.4 104.0 %copy-start.7 = (bf16[64,32]{0,1:T(8,128)(2,1)S(1)}, bf16[64,32]{0,1:T(8,128)(2,1)}, u32[]{:S(2)}) copy-start(bf16[64,32]{0,1:T(8,128)(2,1)} %param.15) | copy-start | bytes 12292
  159.6 441.7 %all-gather.11.cloned.1.call-start = ((), (), s32[]{:S(2)}) async-start(), calls=%async_computation.2 | async-start | bytes 37748736 | tf_op jit(solution)/shard_map/all_gather | solution.py:93
  258.4 14.5 %copy-start.9 = (u32[256]{0:T(256)S(1)}, u32[256]{0:T(256)}, u32[]{:S(2)}) copy-start(u32[256]{0:T(256)} %constant.32) | copy-start | bytes 3076
  258.4 15.8 %copy-start.8 = (s32[64]{0:T(128)S(1)}, s32[64]{0:T(128)}, u32[]{:S(2)}) copy-start(s32[64]{0:T(128)} %param.11) | copy-start | bytes 772
  601.3 14.2 %copy-start.6 = (f32[128]{0:T(128)S(1)}, f32[128]{0:T(128)}, u32[]{:S(2)}) copy-start(f32[128]{0:T(128)} %param.17) | copy-start | bytes 1540
Sparse Core Ops, SparseCore 0:
  9.1 116.6 all-gather.6
  159.7 92.9 all-gather.8
  272.3 328.9 all-gather.10
